TPU v7x, 32 devices: a whole 2x2x4 slice. The times are simulated.
32 devices in a mesh: ctx: 4 (over z), head: 8 (over y, x, core).
Axes of the slice: x: 2, y: 2, z: 4, core: 2. Of those that a mesh axis runs over, the one named last changes fastest.
Arguments:
- layer_input: bfloat16 [1024, 4096], P(('ctx', 'head')), may hold values from -6 to 6
- w_query: bfloat16 [4096, 4096], P('ctx', 'head'), may hold values from -0.09375 to 0.09375
- w_key: bfloat16 [4096, 4096], P('ctx', 'head'), may hold values from -0.09375 to 0.09375
- w_value: bfloat16 [4096, 4096], P('ctx', 'head'), may hold values from -0.09375 to 0.09375
- w_out: bfloat16 [4096, 4096], P('head'), may hold values from -0.09375 to 0.09375
- log_decay: float32 [32, 1024], P('head', 'ctx'), may hold values from -2 to 0
- level_gain: float32 [32, 10], P('head'), may hold values from 0.5 to 2
- level_mask: int32 [8, 10], P('ctx'), may hold values 0 or 1
Outputs:
- layer_out: bfloat16 [1024, 4096], P(('ctx', 'head'))
All inputs are finite; a program needn't handle non-finite values. No bound on the sum of `level_mask` on one device may be relied on, other than what follows from the above.
Results may differ from a plain program's by a relative error of at most 0.023.
Values may be sent and summed in bfloat16 or wider, within the bound.
A program may use at most 64 MiB of HBM per device.

v0:
```python
import jax
import jax.numpy as jnp
from jax import lax
from jax.sharding import PartitionSpec as P

HEAD_DIM = 128
BLOCK = 128


def swapped(value, axis, stride):
    mask = 2**stride
    pairs = [(source, source ^ mask) for source in range(lax.axis_size(axis))]
    return lax.ppermute(value, axis, pairs)


def levels_of(first, second, count):
    mixed = jnp.bitwise_xor(first, second)
    result = jnp.zeros(mixed.shape, jnp.int32)
    for level_bit in range(count):
        result = result + (mixed >= 2**level_bit).astype(jnp.int32)
    return result


def unit_rows(block):
    floated = block.astype(jnp.float32)
    return (floated / jnp.sqrt(jnp.sum(floated * floated, axis=-1, keepdims=True) + 1e-06)).astype(
        jnp.bfloat16
    )


def on_device(layer_input, w_query, w_key, w_value, w_out, log_decay, level_gain, level_mask):
    full_query, full_key, full_value = (
        lax.all_gather(w_query, "ctx", axis=0, tiled=True),
        lax.all_gather(w_key, "ctx", axis=0, tiled=True),
        lax.all_gather(w_value, "ctx", axis=0, tiled=True),
    )
    piece = lax.all_gather(layer_input, "head", axis=0, tiled=True)
    outputs = [
        jnp.dot(piece, weight, preferred_element_type=jnp.float32).astype(jnp.bfloat16)
        for weight in (full_query, full_key, full_value)
    ]
    joined = jnp.concatenate(outputs, axis=1)
    width = full_query.shape[1]
    local_heads = width // HEAD_DIM
    span = joined.shape[0]
    query_unit = unit_rows(joined[:, :width].reshape(span, local_heads, HEAD_DIM))
    key_unit = unit_rows(joined[:, width : 2 * width].reshape(span, local_heads, HEAD_DIM))
    values = joined[:, 2 * width :].reshape(span, local_heads, HEAD_DIM)
    cum = jnp.cumsum(log_decay, axis=1)
    span_total = cum[:, -1]
    level_count = level_gain.shape[1]
    per_span = span // BLOCK
    ctx_index = lax.axis_index("ctx")
    blocks = ctx_index * per_span + jnp.arange(per_span, dtype=jnp.int32)
    level_range = jnp.arange(level_count, dtype=jnp.int32)
    near_levels = levels_of(blocks[:, None], blocks[None, :], level_count)
    near_onehot = (near_levels[..., None] == level_range).astype(jnp.float32)
    block_weight = level_mask.astype(jnp.float32)[:, None, :] * level_gain[None, :, :]
    near_block = jnp.einsum("bhl,bel->hbe", block_weight, near_onehot)
    scores = jnp.einsum("thd,shd->hts", query_unit, key_unit, preferred_element_type=jnp.float32)
    position = jnp.arange(span, dtype=jnp.int32)
    causal = position[:, None] >= position[None, :]
    spread = cum[:, :, None] - cum[:, None, :]
    decay_factor = jnp.where(causal, jnp.exp(jnp.where(causal, spread, 0.0)), 0.0)
    shaped = (scores * decay_factor).reshape(local_heads, per_span, BLOCK, per_span, BLOCK)
    near_weight = (
        (shaped * near_block[:, :, None, :, None])
        .reshape(local_heads, span, span)
        .astype(jnp.bfloat16)
    )
    near_out = jnp.einsum("hts,shd->thd", near_weight, values, preferred_element_type=jnp.float32)
    decayed_key = (
        key_unit.astype(jnp.float32) * jnp.exp(span_total[None, :] - cum.T)[:, :, None]
    ).astype(jnp.bfloat16)
    span_state = jnp.einsum("thd,the->hde", decayed_key, values, preferred_element_type=jnp.float32)
    bit_count = lax.axis_size("ctx").bit_length() - 1
    bit_range = jnp.arange(bit_count, dtype=jnp.int32)
    powers = jnp.left_shift(jnp.ones_like(bit_range), bit_range)
    group_total, group_state = (span_total, span_state)
    before = jnp.zeros_like(span_total)
    collected = []
    for bit_index in range(bit_count):
        other_total, other_state = (
            swapped(group_total.astype(jnp.bfloat16), "ctx", bit_index).astype(group_total.dtype),
            swapped(group_state.astype(jnp.bfloat16), "ctx", bit_index).astype(group_state.dtype),
        )
        upper = jnp.bitwise_and(jnp.right_shift(ctx_index, bit_index), 1) == 1
        collected.append(jnp.where(upper, jnp.exp(before)[:, None, None] * other_state, 0.0))
        lower_total = jnp.where(upper, other_total, group_total)
        higher_total = jnp.where(upper, group_total, other_total)
        lower_state = jnp.where(upper, other_state, group_state)
        higher_state = jnp.where(upper, group_state, other_state)
        group_state = jnp.exp(higher_total)[:, None, None] * lower_state + higher_state
        group_total = lower_total + higher_total
        before = before + jnp.where(upper, other_total, 0.0)
    carried = jnp.stack(collected, axis=0)
    partner = jnp.bitwise_xor(ctx_index, powers)
    far_levels = levels_of(blocks[:, None], (partner * per_span)[None, :], level_count)
    far_onehot = (far_levels[..., None] == level_range).astype(jnp.float32)
    far_block = jnp.einsum("bhl,bml->bhm", block_weight, far_onehot)
    far_tokens = jnp.repeat(far_block, BLOCK, axis=0)
    scaled = query_unit.astype(jnp.float32) * jnp.exp(cum.T)[:, :, None]
    reached = jnp.einsum("thd,mhde->thme", scaled, carried, precision=lax.Precision.HIGHEST)
    far_out = jnp.einsum("thme,thm->the", reached, far_tokens, precision=lax.Precision.HIGHEST)
    heads_out = (near_out + far_out).astype(jnp.bfloat16).reshape(span, width)
    return lax.psum_scatter(
        jnp.dot(heads_out, w_out, preferred_element_type=jnp.float32).astype(jnp.bfloat16),
        "head",
        scatter_dimension=0,
        tiled=True,
    )


def solution(mesh):
    in_specs = (
        P(("ctx", "head"), None),
        P("ctx", "head"),
        P("ctx", "head"),
        P("ctx", "head"),
        P("head", None),
        P("head", "ctx"),
        P("head", None),
        P("ctx", None),
    )
    out_specs = P(("ctx", "head"), None)
    return jax.shard_map(
        on_device, mesh=mesh, in_specs=in_specs, out_specs=out_specs, check_vma=False
    )
```

profile of v0, /device:TPU:0, one launch (start us, length us, event | category | flops | bytes accessed | tf_op | source)
XLA Modules:
  0.0 354.7 jit_solution(5729758578422168812)
XLA Ops:
  6.5 0.7 all-gather.5.cloned.1.call-update
  7.3 0.7 all-gather.9.cloned.1.call-update
  8.1 0.7 all-gather.11.cloned.1.call-update
  8.8 0.5 all-gather.7.cloned.1.call-update
  9.4 0.7 reshape.199
  10.1 1.2 reduce-window.6
  11.8 3.1 collective-permute-start.1
  14.9 0.7 convert_element_type.227
  15.7 0.9 convolution_bitcast_fusion.2
  17.0 0.9 fusion.33
  18.0 0.2 copy.40
  18.2 0.3 mul.82
  18.5 0.8 mul.83
  19.4 20.3 %all-gather.5.cloned.1.call-done = bf16[256,4096]{1,0:T(8,128)(2,1)} async-done(((bf16[32,4096]{1,0:T(8,128)(2,1)}), bf16[256,4096]{1,0:T(8,128)(2,1)}) %all-gather.5.cloned.1.call-update) | async-done | bytes 2097168 | tf_op jit(solution)/shard_map/all_gather | solution.py:37
  39.8 82.3 %all-gather.9.cloned.1.call-done = bf16[4096,512]{1,0:T(8,128)(2,1)} async-done(((bf16[1024,512]{1,0:T(8,128)(2,1)}), bf16[4096,512]{1,0:T(8,128)(2,1)}) %all-gather.9.cloned.1.call-update) | async-done | bytes 4194320 | tf_op jit(solution)/shard_map/all_gather | solution.py:33
  122.1 4.1 %fusion.7 = f32[256,512]{1,0:T(8,128)S(1)} fusion(bf16[256,4096]{1,0:T(8,128)(2,1)} %all-gather.5.cloned.1.call-done, bf16[4096,512]{1,0:T(8,128)(2,1)} %all-gather.9.cloned.1.call-done), kind=kOutput, calls=%fused_computation.13 | convolution fusion | flops 1074003968 | bytes 6815744 | tf_op jit(solution)/shard_map/dot_general | solution.py:39
  126.3 76.6 %all-gather.11.cloned.1.call-done = bf16[4096,512]{1,0:T(8,128)(2,1)} async-done(((bf16[1024,512]{1,0:T(8,128)(2,1)}), bf16[4096,512]{1,0:T(8,128)(2,1)}) %all-gather.11.cloned.1.call-update) | async-done | bytes 4194320 | tf_op jit(solution)/shard_map/all_gather | solution.py:34
  202.9 4.1 %fusion.6 = f32[256,512]{1,0:T(8,128)S(1)} fusion(bf16[256,4096]{1,0:T(8,128)(2,1)} %all-gather.5.cloned.1.call-done, bf16[4096,512]{1,0:T(8,128)(2,1)} %all-gather.11.cloned.1.call-done), kind=kOutput, calls=%fused_computation.11 | convolution fusion | flops 1074003968 | bytes 6815744 | tf_op jit(solution)/shard_map/dot_general | solution.py:39
  207.2 0.3 multiply_reduce_fusion
  207.5 0.3 multiply_reduce_fusion.1
  207.9 0.7 multiply_convert_fusion
  208.6 75.0 %all-gather.7.cloned.1.call-done = bf16[4096,512]{1,0:T(8,128)(2,1)} async-done(((bf16[1024,512]{1,0:T(8,128)(2,1)}), bf16[4096,512]{1,0:T(8,128)(2,1)}) %all-gather.7.cloned.1.call-update) | async-done | bytes 4194320 | tf_op jit(solution)/shard_map/all_gather | solution.py:35
  283.6 4.1 %fusion.8 = bf16[32,4,8,128]{3,2,1,0:T(8,128)(2,1)S(1)} fusion(bf16[256,4096]{1,0:T(8,128)(2,1)} %all-gather.5.cloned.1.call-done, bf16[4096,512]{1,0:T(8,128)(2,1)} %all-gather.7.cloned.1.call-done), kind=kOutput, calls=%fused_computation.15 | convolution fusion | flops 1073872896 | bytes 6553600 | tf_op jit(solution)/shard_map/dot_general | solution.py:39
  287.7 0.3 fusion.87
  288.1 5.0 %collective-permute-done = bf16[4,128,128]{2,1,0:T(8,128)(2,1)S(1)} collective-permute-done((bf16[4,128,128]{2,1,0:T(8,128)(2,1)S(1)}, bf16[4,128,128]{2,1,0:T(8,128)(2,1)S(1)}, u32[]{:S(2)}, u32[]{:S(2)}) %collective-permute-start) | collective-permute-done | bytes 131104 | tf_op jit(solution)/shard_map/ppermute | solution.py:13
  293.2 0.9 collective-permute-start.2
  294.2 0.7 multiply_bitcast_fusion
  294.9 6.4 %collective-permute-done.2 = bf16[4,128,128]{2,1,0:T(8,128)(2,1)S(1)} collective-permute-done((bf16[4,128,128]{2,1,0:T(8,128)(2,1)S(1)}, bf16[4,128,128]{2,1,0:T(8,128)(2,1)S(1)}, u32[]{:S(2)}, u32[]{:S(2)}) %collective-permute-start.2) | collective-permute-done | bytes 131104 | tf_op jit(solution)/shard_map/ppermute | solution.py:13
  301.3 1.1 fusion.3
  302.4 0.6 fusion.5
  303.0 4.8 %convolution_convert_fusion = bf16[256,4096]{1,0:T(8,128)(2,1)} fusion(bf16[256,512]{0,1:T(8,128)(2,1)S(1)} %bitcast.57, bf16[512,4096]{1,0:T(8,128)(2,1)} %param.12), kind=kOutput, calls=%fused_computation | convolution fusion | flops 1074790400 | bytes 6553600 | tf_op jit(solution)/shard_map/dot_general | solution.py:107
  307.9 40.3 %reduce-scatter.2.cloned.1.call-done = bf16[32,4096]{1,0:T(8,128)(2,1)} async-done(((bf16[256,4096]{1,0:T(8,128)(2,1)}), bf16[32,4096]{1,0:T(8,128)(2,1)}) %reduce-scatter.2.cloned.1.call-update) | async-done | bytes 262160 | tf_op jit(solution)/shard_map/reduce_scatter | solution.py:106
  (33 shorter events, 2.1 us)
Async XLA Ops:
  6.5 33.2 %all-gather.5.cloned.1.call-start = ((), (), s32[]{:S(2)}) async-start(), calls=%async_computation.1 | async-start | bytes 2359296 | tf_op jit(solution)/shard_map/all_gather | solution.py:37
  7.3 114.8 %all-gather.9.cloned.1.call-start = ((), (), s32[]{:S(2)}) async-start(), calls=%async_computation.3 | async-start | bytes 5242880 | tf_op jit(solution)/shard_map/all_gather | solution.py:33
  8.0 194.9 %all-gather.11.cloned.1.call-start = ((), (), s32[]{:S(2)}) async-start(), calls=%async_computation.4 | async-start | bytes 5242880 | tf_op jit(solution)/shard_map/all_gather | solution.py:34
  8.7 274.9 %all-gather.7.cloned.1.call-start = ((), (), s32[]{:S(2)}) async-start(), calls=%async_computation.2 | async-start | bytes 5242880 | tf_op jit(solution)/shard_map/all_gather | solution.py:35
  9.3 338.8 %reduce-scatter.2.cloned.1.call-start = ((), (), s32[]{:S(2)}) async-start(), calls=%async_computation.5 | async-start | bytes 2359296 | tf_op jit(solution)/shard_map/reduce_scatter | solution.py:106
  11.8 7.6 %collective-permute-start.1 = (bf16[4]{0:T(256)(128)(2,1)S(1)}, bf16[4]{0:T(256)(128)(2,1)S(1)}, u32[]{:S(2)}, u32[]{:S(2)}) collective-permute-start(bf16[4]{0:T(256)(128)(2,1)S(1)} %bitcast_convert_fusion), channel_id=1, source_target_pairs={{0,8},{8,0},{16,24},{24,16},{1,9},{9,1},{17,25},{25,17},{2,10},{10... | collective-permute-start | bytes 32 | tf_op jit(solution)/shard_map/ppermute | solution.py:13
  288.0 5.2 %collective-permute-start = (bf16[4,128,128]{2,1,0:T(8,128)(2,1)S(1)}, bf16[4,128,128]{2,1,0:T(8,128)(2,1)S(1)}, u32[]{:S(2)}, u32[]{:S(2)}) collective-permute-start(bf16[4,128,128]{2,1,0:T(8,128)(2,1)S(1)} %get-tuple-element.17), channel_id=1, source_target_pairs={{0,8},{8,0},{16,24},{24,16},{1,9},{9,1},{17,25},{25,17},{2,10},{10... | collective-permute-start | bytes 393224 | tf_op jit(solution)/shard_map/ppermute | solution.py:13
  293.2 8.0 %collective-permute-start.2 = (bf16[4,128,128]{2,1,0:T(8,128)(2,1)S(1)}, bf16[4,128,128]{2,1,0:T(8,128)(2,1)S(1)}, u32[]{:S(2)}, u32[]{:S(2)}) collective-permute-start(bf16[4,128,128]{2,1,0:T(8,128)(2,1)S(1)} %get-tuple-element.10), channel_id=1, source_target_pairs={{0,16},{8,24},{16,0},{24,8},{1,17},{9,25},{17,1},{25,9},{2,18},{10... | collective-permute-start | bytes 393224 | tf_op jit(solution)/shard_map/ppermute | solution.py:13
Sparse Core Ops, SparseCore 0:
  9.2 30.4 all-gather.4
  41.3 80.7 all-gather.8
  123.7 79.2 all-gather.10
  204.3 79.2 all-gather.6
  308.0 40.1 reduce-scatter.1
where the time goes:
time: 355 us
  waiting for transfers between devices  308 us (87%)
  matrix products  20.7 us (6%)
  between operations  13.3 us (4%)
  other arithmetic  4.58 us (1%)
  starting transfers between devices  4.23 us (1%)
    all_gather x1, waiting for transfers between devices, on_device(): lax.all_gather(w_query, 'ctx', axis=0, tiled=True)  82.3 us
    all_gather x1, waiting for transfers between devices, on_device(): lax.all_gather(w_key, 'ctx', axis=0, tiled=True)  76.6 us
    all_gather x1, waiting for transfers between devices, on_device(): lax.all_gather(w_value, 'ctx', axis=0, tiled=True)  75 us
    reduce_scatter x1, waiting for transfers between devices, on_device(): lax.psum_scatter(jnp.dot(heads_out, w_out, preferred_element_type=jnp.flo...  40.3 us
    all_gather x1, waiting for transfers between devices, on_device(): piece = lax.all_gather(layer_input, 'head', axis=0, tiled=True)  20.3 us
    dot_general x3, matrix products, on_device(): jnp.dot(piece, weight, preferred_element_type=jnp.float32)  12.2 us
    ppermute x3, waiting for transfers between devices, swapped(): return lax.ppermute(value, axis, pairs)  11.4 us
  transfers between devices with their start and end apart: 8, of which 7 were waited for; matrix products, arithmetic and copies ran while one was open for 5% of the time, Pallas kernels for 0%

commit v1 on v0

--- a/solution.py
+++ b/solution.py
@@ -5,6 +5,23 @@
 
 HEAD_DIM = 128
 BLOCK = 128
+
+
+def in_order(blocks, dim):
+    blocks = jnp.moveaxis(blocks, 0, dim)
+    shape = blocks.shape
+    return blocks.reshape(*shape[:dim], shape[dim] * shape[dim + 1], *shape[dim + 2 :])
+
+
+def gather_around(x, axis, dim):
+    size = lax.axis_size(axis)
+    ahead = [(i, (i + 1) % size) for i in range(size)]
+    blocks = [x]
+    while len(blocks) < size:
+        blocks.append(lax.ppermute(blocks[-1], axis, ahead))
+    index = lax.axis_index(axis)
+    blocks = jnp.stack(blocks)[(index - jnp.arange(size)) % size]
+    return in_order(blocks, dim)
 
 
 def swapped(value, axis, stride):
@@ -30,7 +47,7 @@
 
 def on_device(layer_input, w_query, w_key, w_value, w_out, log_decay, level_gain, level_mask):
     full_query, full_key, full_value = (
-        lax.all_gather(w_query, "ctx", axis=0, tiled=True),
+        gather_around(w_query, "ctx", 0),
         lax.all_gather(w_key, "ctx", axis=0, tiled=True),
         lax.all_gather(w_value, "ctx", axis=0, tiled=True),
     )

time: 355 us -> 306 us (0.86)
  waiting for transfers between devices: 308 us -> 248 us
  starting transfers between devices: 4.23 us -> 10.9 us
  local copies, waits for them, and re-layouts: 3.36 us -> 8.11 us
    ppermute x0 -> x3, waiting for transfers between devices: none -> 103 us  [gather_around(): blocks.append(lax.ppermute(blocks[-1], axis, ahead))]
    all_gather x1 -> x0, waiting for transfers between devices: 82.3 us -> none  [on_device(): lax.all_gather(w_query, 'ctx', axis=0, tiled=True)]
    all_gather x1, waiting for transfers between devices: 76.6 us -> 16.4 us  [on_device(): lax.all_gather(w_key, 'ctx', axis=0, tiled=True)]
    all_gather x1, waiting for transfers between devices: 20.3 us -> 0.01 us  [on_device(): piece = lax.all_gather(layer_input, 'head', axis=0, tiled=True)]
    ppermute x0 -> x3, starting transfers between devices: none -> 8.49 us  [gather_around(): blocks.append(lax.ppermute(blocks[-1], axis, ahead))]
    gather x0 -> x1, local copies, waits for them, and re-layouts: none -> 4.93 us  [gather_around(): blocks = jnp.stack(blocks)[(index - jnp.arange(size)) % size]]
    another operation x2 -> x3, other arithmetic: 1.24 us -> 4.87 us  [the longest x1 3.62 us: gather_around(): blocks = jnp.stack(blocks)[(index - jnp.arange(size)) % size]]
  transfers between devices with their start and end apart: 8 -> 10, of which waited for: 7 -> 8; matrix products, arithmetic and copies ran while one was open for 5% -> 7% of each run, Pallas kernels for 0% -> 0%
where the time goes in v1:
time: 306 us
  waiting for transfers between devices  248 us (81%)
  matrix products  18.2 us (6%)
  between operations  13.3 us (4%)
  starting transfers between devices  10.9 us (4%)
  local copies, waits for them, and re-layouts  8.11 us (3%)
  other arithmetic  7.15 us (2%)
    ppermute x3, waiting for transfers between devices, gather_around(): blocks.append(lax.ppermute(blocks[-1], axis, ahead))  103 us
    all_gather x1, waiting for transfers between devices, on_device(): lax.all_gather(w_value, 'ctx', axis=0, tiled=True)  75.1 us
    reduce_scatter x1, waiting for transfers between devices, on_device(): lax.psum_scatter(jnp.dot(heads_out, w_out, preferred_element_type=jnp.flo...  40.3 us
    all_gather x1, waiting for transfers between devices, on_device(): lax.all_gather(w_key, 'ctx', axis=0, tiled=True)  16.4 us
    ppermute x3, waiting for transfers between devices, swapped(): return lax.ppermute(value, axis, pairs)  10.7 us
    dot_general x3, matrix products, on_device(): jnp.dot(piece, weight, preferred_element_type=jnp.float32)  9.6 us
    ppermute x3, starting transfers between devices, gather_around(): blocks.append(lax.ppermute(blocks[-1], axis, ahead))  8.49 us
  transfers between devices with their start and end apart: 10, of which 8 were waited for; matrix products, arithmetic and copies ran while one was open for 7% of the time, Pallas kernels for 0%

profile of v1, /device:TPU:0, one launch (start us, length us, event | category | flops | bytes accessed | tf_op | source)
XLA Modules:
  0.0 305.5 jit_solution(434607616284865945)
XLA Ops:
  6.5 0.7 all-gather.4.cloned.1.call-update
  7.3 0.7 all-gather.8.cloned.1.call-update
  8.1 0.7 all-gather.6.cloned.1.call-update
  8.8 3.1 %collective-permute-start = (bf16[1024,512]{1,0:T(8,128)(2,1)}, bf16[1024,512]{1,0:T(8,128)(2,1)S(1)}, u32[]{:S(2)}, u32[]{:S(2)}) collective-permute-start(bf16[1024,512]{1,0:T(8,128)(2,1)} %param.9), channel_id=1, source_target_pairs={{0,8},{8,16},{16,24},{24,0},{1,9},{9,17},{17,25},{25,1},{2,10},{10... | collective-permute-start | bytes 3145736 | tf_op jit(solution)/shard_map/ppermute | solution.py:21
  11.9 25.4 %collective-permute-done = bf16[1024,512]{1,0:T(8,128)(2,1)S(1)} collective-permute-done((bf16[1024,512]{1,0:T(8,128)(2,1)}, bf16[1024,512]{1,0:T(8,128)(2,1)S(1)}, u32[]{:S(2)}, u32[]{:S(2)}) %collective-permute-start) | collective-permute-done | bytes 1048608 | tf_op jit(solution)/shard_map/ppermute | solution.py:21
  37.3 0.7 reshape.252
  38.0 1.2 reduce-window.6
  39.8 1.3 collective-permute-start.4
  41.1 0.7 convert_element_type.232
  41.8 32.6 %collective-permute-done.1 = bf16[1024,512]{1,0:T(8,128)(2,1)} collective-permute-done((bf16[1024,512]{1,0:T(8,128)(2,1)S(1)}, bf16[1024,512]{1,0:T(8,128)(2,1)}, u32[]{:S(2)}, u32[]{:S(2)}) %collective-permute-start.1) | collective-permute-done | bytes 1048608 | tf_op jit(solution)/shard_map/ppermute | solution.py:21
  74.5 5.4 %collective-permute-start.2 = (bf16[1024,512]{1,0:T(8,128)(2,1)}, bf16[1024,512]{1,0:T(8,128)(2,1)}, u32[]{:S(2)}, u32[]{:S(2)}) collective-permute-start(bf16[1024,512]{1,0:T(8,128)(2,1)} %collective-permute-done.1), channel_id=1, source_target_pairs={{0,8},{8,16},{16,24},{24,0},{1,9},{9,17},{17,25},{25,1},{2,10},{10... | collective-permute-start | bytes 3145736 | tf_op jit(solution)/shard_map/ppermute | solution.py:21
  79.9 0.9 fusion.34
  81.3 0.9 convolution_bitcast_fusion.2
  82.2 0.3 mul.82
  82.6 0.8 mul.83
  83.5 45.3 %collective-permute-done.2 = bf16[1024,512]{1,0:T(8,128)(2,1)} collective-permute-done((bf16[1024,512]{1,0:T(8,128)(2,1)}, bf16[1024,512]{1,0:T(8,128)(2,1)}, u32[]{:S(2)}, u32[]{:S(2)}) %collective-permute-start.2) | collective-permute-done | bytes 1048608 | tf_op jit(solution)/shard_map/ppermute | solution.py:21
  128.9 3.6 %pad_maximum_fusion = bf16[4,1024,512]{2,1,0:T(8,128)(2,1)} fusion(bf16[1,1024,512]{2,1,0:T(8,128)(2,1)} %bitcast.3, bf16[1,1024,512]{2,1,0:T(8,128)(2,1)} %bitcast.2, bf16[1,1024,512]{2,1,0:T(8,128)(2,1)} %bitcast.79, bf16[1,1024,512]{2,1,0:T(8,128)(2,1)S(1)} %bitcast.78), kind=kLoop, calls=%fused_computation.2 | loop fusion | flops 6291456 | bytes 8388608 | tf_op jit(solution)/shard_map/stack | solution.py:23
  132.5 4.9 %gather_fusion = bf16[4,1024,512]{2,1,0:T(8,128)(2,1)} fusion(bf16[4,1024,512]{2,1,0:T(8,128)(2,1)} %pad_maximum_fusion, s32[1024]{0:T(1024)S(1)} %pad_clamp_fusion), kind=kCustom, calls=%fused_computation | custom fusion | bytes 8388624 | tf_op jit(solution)/shard_map/gather | solution.py:23
  137.4 16.4 %all-gather.8.cloned.1.call-done = bf16[4096,512]{1,0:T(8,128)(2,1)} async-done(((bf16[1024,512]{1,0:T(8,128)(2,1)}), bf16[4096,512]{1,0:T(8,128)(2,1)}) %all-gather.8.cloned.1.call-update) | async-done | bytes 4194320 | tf_op jit(solution)/shard_map/all_gather | solution.py:51
  153.8 4.1 %fusion.6 = f32[256,512]{1,0:T(8,128)S(1)} fusion(bf16[256,4096]{1,0:T(8,128)(2,1)} %all-gather.4.cloned.1.call-done, bf16[4096,512]{1,0:T(8,128)(2,1)} %all-gather.8.cloned.1.call-done), kind=kOutput, calls=%fused_computation.13 | convolution fusion | flops 1074003968 | bytes 6815744 | tf_op jit(solution)/shard_map/dot_general | solution.py:56
  158.1 0.3 multiply_reduce_fusion
  158.5 0.7 multiply_convert_fusion
  159.2 75.1 %all-gather.6.cloned.1.call-done = bf16[4096,512]{1,0:T(8,128)(2,1)} async-done(((bf16[1024,512]{1,0:T(8,128)(2,1)}), bf16[4096,512]{1,0:T(8,128)(2,1)}) %all-gather.6.cloned.1.call-update) | async-done | bytes 4194320 | tf_op jit(solution)/shard_map/all_gather | solution.py:52
  234.3 4.2 %fusion.8 = bf16[32,4,8,128]{3,2,1,0:T(8,128)(2,1)S(1)} fusion(bf16[256,4096]{1,0:T(8,128)(2,1)} %all-gather.4.cloned.1.call-done, bf16[4096,512]{1,0:T(8,128)(2,1)} %all-gather.6.cloned.1.call-done), kind=kOutput, calls=%fused_computation.17 | convolution fusion | flops 1073872896 | bytes 6553600 | tf_op jit(solution)/shard_map/dot_general | solution.py:56
  239.0 1.3 multiply_reduce_fusion.1
  240.3 3.6 %collective-permute-done.3 = bf16[4,128,128]{2,1,0:T(8,128)(2,1)S(1)} collective-permute-done((bf16[4,128,128]{2,1,0:T(8,128)(2,1)S(1)}, bf16[4,128,128]{2,1,0:T(8,128)(2,1)S(1)}, u32[]{:S(2)}, u32[]{:S(2)}) %collective-permute-start.3) | collective-permute-done | bytes 131104 | tf_op jit(solution)/shard_map/ppermute | solution.py:30
  244.0 0.9 collective-permute-start.5
  245.0 7.1 %collective-permute-done.5 = bf16[4,128,128]{2,1,0:T(8,128)(2,1)S(1)} collective-permute-done((bf16[4,128,128]{2,1,0:T(8,128)(2,1)S(1)}, bf16[4,128,128]{2,1,0:T(8,128)(2,1)S(1)}, u32[]{:S(2)}, u32[]{:S(2)}) %collective-permute-start.5) | collective-permute-done | bytes 131104 | tf_op jit(solution)/shard_map/ppermute | solution.py:30
  252.1 1.1 fusion.3
  253.2 0.7 fusion.5
  253.9 4.8 %convolution_convert_fusion = bf16[256,4096]{1,0:T(8,128)(2,1)} fusion(bf16[256,512]{0,1:T(8,128)(2,1)S(1)} %bitcast.80, bf16[512,4096]{1,0:T(8,128)(2,1)} %param.12), kind=kOutput, calls=%fused_computation.1 | convolution fusion | flops 1074790400 | bytes 6553600 | tf_op jit(solution)/shard_map/dot_general | solution.py:124
  258.7 40.3 %reduce-scatter.2.cloned.1.call-done = bf16[32,4096]{1,0:T(8,128)(2,1)} async-done(((bf16[256,4096]{1,0:T(8,128)(2,1)}), bf16[32,4096]{1,0:T(8,128)(2,1)}) %reduce-scatter.2.cloned.1.call-update) | async-done | bytes 262160 | tf_op jit(solution)/shard_map/reduce_scatter | solution.py:123
  (44 shorter events, 2.4 us)
Async XLA Ops:
  6.5 122.3 %copy-start.1 = (bf16[1024,512]{1,0:T(8,128)(2,1)S(1)}, bf16[1024,512]{1,0:T(8,128)(2,1)}, u32[]{:S(2)}) copy-start(bf16[1024,512]{1,0:T(8,128)(2,1)} %param.9) | copy-start | bytes 3145732
  6.5 130.9 %all-gather.4.cloned.1.call-start = ((), (), s32[]{:S(2)}) async-start(), calls=%async_computation.1 | async-start | bytes 2359296 | tf_op jit(solution)/shard_map/all_gather | solution.py:54
  7.3 146.6 %all-gather.8.cloned.1.call-start = ((), (), s32[]{:S(2)}) async-start(), calls=%async_computation.3 | async-start | bytes 5242880 | tf_op jit(solution)/shard_map/all_gather | solution.py:51
  8.0 226.2 %all-gather.6.cloned.1.call-start = ((), (), s32[]{:S(2)}) async-start(), calls=%async_computation.2 | async-start | bytes 5242880 | tf_op jit(solution)/shard_map/all_gather | solution.py:52
  8.7 290.2 %reduce-scatter.2.cloned.1.call-start = ((), (), s32[]{:S(2)}) async-start(), calls=%async_computation.4 | async-start | bytes 2359296 | tf_op jit(solution)/shard_map/reduce_scatter | solution.py:123
  8.8 28.5 %collective-permute-start = (bf16[1024,512]{1,0:T(8,128)(2,1)}, bf16[1024,512]{1,0:T(8,128)(2,1)S(1)}, u32[]{:S(2)}, u32[]{:S(2)}) collective-permute-start(bf16[1024,512]{1,0:T(8,128)(2,1)} %param.9), channel_id=1, source_target_pairs={{0,8},{8,16},{16,24},{24,0},{1,9},{9,17},{17,25},{25,1},{2,10},{10... | collective-permute-start | bytes 3145736 | tf_op jit(solution)/shard_map/ppermute | solution.py:21
  37.3 42.6 %copy-start.2 = (bf16[1024,512]{1,0:T(8,128)(2,1)}, bf16[1024,512]{1,0:T(8,128)(2,1)S(1)}, u32[]{:S(2)}) copy-start(bf16[1024,512]{1,0:T(8,128)(2,1)S(1)} %collective-permute-done) | copy-start | bytes 3145732
  37.3 37.2 %collective-permute-start.1 = (bf16[1024,512]{1,0:T(8,128)(2,1)S(1)}, bf16[1024,512]{1,0:T(8,128)(2,1)}, u32[]{:S(2)}, u32[]{:S(2)}) collective-permute-start(bf16[1024,512]{1,0:T(8,128)(2,1)S(1)} %collective-permute-done), channel_id=1, source_target_pairs={{0,8},{8,16},{16,24},{24,0},{1,9},{9,17},{17,25},{25,1},{2,10},{10... | collective-permute-start | bytes 3145736 | tf_op jit(solution)/shard_map/ppermute | solution.py:21
  39.8 43.7 %collective-permute-start.4 = (bf16[4]{0:T(256)(128)(2,1)S(1)}, bf16[4]{0:T(256)(128)(2,1)S(1)}, u32[]{:S(2)}, u32[]{:S(2)}) collective-permute-start(bf16[4]{0:T(256)(128)(2,1)S(1)} %bitcast_convert_fusion), channel_id=1, source_target_pairs={{0,8},{8,0},{16,24},{24,16},{1,9},{9,1},{17,25},{25,17},{2,10},{10... | collective-permute-start | bytes 32 | tf_op jit(solution)/shard_map/ppermute | solution.py:30
  74.5 54.4 %collective-permute-start.2 = (bf16[1024,512]{1,0:T(8,128)(2,1)}, bf16[1024,512]{1,0:T(8,128)(2,1)}, u32[]{:S(2)}, u32[]{:S(2)}) collective-permute-start(bf16[1024,512]{1,0:T(8,128)(2,1)} %collective-permute-done.1), channel_id=1, source_target_pairs={{0,8},{8,16},{16,24},{24,0},{1,9},{9,17},{17,25},{25,1},{2,10},{10... | collective-permute-start | bytes 3145736 | tf_op jit(solution)/shard_map/ppermute | solution.py:21
  234.2 4.6 %copy-start = (bf16[4,1024,512]{2,1,0:T(8,128)(2,1)S(1)}, bf16[4,1024,512]{2,1,0:T(8,128)(2,1)}, u32[]{:S(2)}) copy-start(bf16[4,1024,512]{2,1,0:T(8,128)(2,1)} %gather_fusion) | copy-start | bytes 12582916
  234.3 4.7 %copy-start.3 = (bf16[256,4096]{1,0:T(8,128)(2,1)S(1)}, bf16[256,4096]{1,0:T(8,128)(2,1)}, u32[]{:S(2)}) copy-start(bf16[256,4096]{1,0:T(8,128)(2,1)} %all-gather.4.cloned.1.call-done) | copy-start | bytes 6291460
  238.7 5.2 %collective-permute-start.3 = (bf16[4,128,128]{2,1,0:T(8,128)(2,1)S(1)}, bf16[4,128,128]{2,1,0:T(8,128)(2,1)S(1)}, u32[]{:S(2)}, u32[]{:S(2)}) collective-permute-start(bf16[4,128,128]{2,1,0:T(8,128)(2,1)S(1)} %get-tuple-element.15), channel_id=1, source_target_pairs={{0,8},{8,0},{16,24},{24,16},{1,9},{9,1},{17,25},{25,17},{2,10},{10... | collective-permute-start | bytes 393224 | tf_op jit(solution)/shard_map/ppermute | solution.py:30
  244.0 8.0 %collective-permute-start.5 = (bf16[4,128,128]{2,1,0:T(8,128)(2,1)S(1)}, bf16[4,128,128]{2,1,0:T(8,128)(2,1)S(1)}, u32[]{:S(2)}, u32[]{:S(2)}) collective-permute-start(bf16[4,128,128]{2,1,0:T(8,128)(2,1)S(1)} %get-tuple-element.8), channel_id=1, source_target_pairs={{0,16},{8,24},{16,0},{24,8},{1,17},{9,25},{17,1},{25,9},{2,18},{10... | collective-permute-start | bytes 393224 | tf_op jit(solution)/shard_map/ppermute | solution.py:30
Sparse Core Ops, SparseCore 0:
  9.2 30.5 all-gather.3
  41.4 112.3 all-gather.7
  155.4 78.8 all-gather.5
  258.8 40.1 reduce-scatter.1
